TPU v7x, 32 devices: a whole 2x2x4 slice. The times are simulated.
32 devices in a mesh: blk: 4 (over y, x), ep: 8 (over z, core).
Axes of the slice: x: 2, y: 2, z: 4, core: 2. Of those that a mesh axis runs over, the one named last changes fastest.
Arguments:
- tokens: bfloat16 [4096, 1024], P(('blk', 'ep')), may hold values from -6 to 6
- expert_ids: int32 [4096, 6], P(('blk', 'ep')), may hold values from 0 to 63, all different within a row; in each aligned block of 128 rows (0 to 127, 128 to 255, ...) at most 16 rows name the same one
- route_weight: float32 [4096, 6], P(('blk', 'ep')), may hold values from 0.05 to 1
- gate_weight: bfloat16 [1024, 64, 768], P('blk', 'ep'), may hold values from -0.1875 to 0.1875
- up_weight: bfloat16 [1024, 64, 768], P('blk', 'ep'), may hold values from -0.1875 to 0.1875
- down_weight: bfloat16 [1024, 64, 768], P('blk', 'ep'), may hold values from -0.21875 to 0.21875
- out_grad: bfloat16 [4096, 1024], P(('blk', 'ep')), may hold values from -6 to 6
Outputs:
- layer_output: bfloat16 [4096, 1024], P(('blk', 'ep'))
- grad_tokens: float32 [4096, 1024], P(('blk', 'ep'))
- grad_route: float32 [4096, 6], P(('blk', 'ep'))
- grad_gate: float32 [1024, 64, 768], P('blk', 'ep')
- grad_up: float32 [1024, 64, 768], P('blk', 'ep')
- grad_down: float32 [1024, 64, 768], P('blk', 'ep')
Inputs may be any that keep to these rules, and one draw needn't show every extreme that they name: `expert_ids`: within the 128 tokens of one device, the 6 experts of a token differ, and no expert is named by more than 16 of them; in every draw some expert is named by exactly 16 tokens of some device.
All inputs are finite; a program needn't handle non-finite values.
Results may differ from a plain program's by a relative error of at most 0.008.
Values may be sent and summed in bfloat16 or wider, within the bound.
No kernel may reach another device: no remote copies, remote signals or barrier semaphores. Data moves between devices by JAX's collectives and lax.ppermute only.
A program may use at most 256 MiB of HBM per device.

v0:
```python
import jax
import jax.numpy as jnp
from jax import lax
from jax.sharding import PartitionSpec as P

EXPERTS = 64
CAP = 16


def expand_rows(routed, weights):
    return jnp.einsum("erd,def->erf", routed, weights, preferred_element_type=jnp.float32)


def contract_rows(inner, weights):
    return jnp.einsum("erf,def->erd", inner, weights, preferred_element_type=jnp.float32)


def outer_rows(routed, inner):
    return jnp.einsum("erd,erf->def", routed, inner, preferred_element_type=jnp.float32)


def body(tokens, expert_ids, route_weight, gate_weight, up_weight, down_weight, out_grad):
    tok_count, model_width = tokens.shape
    top_count = expert_ids.shape[1]
    experts = EXPERTS
    capacity = CAP
    flat_ids = expert_ids.reshape(-1)
    onehot = (flat_ids[:, None] == jnp.arange(experts, dtype=jnp.int32)[None, :]).astype(jnp.int32)
    slot_rank = jnp.sum((jnp.cumsum(onehot, axis=0) - 1) * onehot, axis=1)
    target = flat_ids * capacity + slot_rank
    repeated = jnp.repeat(tokens, top_count, axis=0)
    outgoing = jnp.zeros((experts * capacity, model_width), jnp.bfloat16).at[target].set(repeated)
    received = lax.all_to_all(
        outgoing.reshape(experts, capacity, model_width),
        "ep",
        split_axis=0,
        concat_axis=1,
        tiled=True,
    )
    gate_full, up_full, down_full = (
        lax.all_gather(gate_weight, "blk", axis=0, tiled=True),
        lax.all_gather(up_weight, "blk", axis=0, tiled=True),
        lax.all_gather(down_weight, "blk", axis=0, tiled=True),
    )
    gate_pre = expand_rows(received, gate_full)
    up_pre = expand_rows(received, up_full)
    gate_sig = jax.nn.sigmoid(gate_pre)
    hidden = (gate_pre * gate_sig * up_pre).astype(jnp.bfloat16)
    expert_out = contract_rows(hidden, down_full).astype(jnp.bfloat16)
    returned = lax.all_to_all(expert_out, "ep", split_axis=1, concat_axis=0, tiled=True)
    chosen = returned.reshape(experts * capacity, model_width)[target].reshape(
        tok_count, top_count, model_width
    )
    chosen_f32 = chosen.astype(jnp.float32)
    layer_output = jnp.sum(route_weight[:, :, None] * chosen_f32, axis=1).astype(jnp.bfloat16)
    grad_f32 = out_grad.astype(jnp.float32)
    grad_route = jnp.sum(chosen_f32 * grad_f32[:, None, :], axis=2)
    slot_grad = (route_weight[:, :, None] * grad_f32[:, None, :]).astype(jnp.bfloat16)
    grad_send = (
        jnp.zeros((experts * capacity, model_width), jnp.bfloat16)
        .at[target]
        .set(slot_grad.reshape(-1, model_width))
    )
    grad_recv = lax.all_to_all(
        grad_send.reshape(experts, capacity, model_width),
        "ep",
        split_axis=0,
        concat_axis=1,
        tiled=True,
    )
    down_summed = lax.psum_scatter(
        outer_rows(grad_recv, hidden).astype(jnp.bfloat16), "blk", scatter_dimension=0, tiled=True
    ).astype(jnp.float32)
    grad_hidden = expand_rows(grad_recv, down_full)
    gate_delta = (grad_hidden * up_pre * gate_sig * (1.0 + gate_pre * (1.0 - gate_sig))).astype(
        jnp.bfloat16
    )
    up_delta = (grad_hidden * gate_pre * gate_sig).astype(jnp.bfloat16)
    input_grad = (contract_rows(gate_delta, gate_full) + contract_rows(up_delta, up_full)).astype(
        jnp.bfloat16
    )
    grad_back = lax.all_to_all(input_grad, "ep", split_axis=1, concat_axis=0, tiled=True)
    picked_grad = grad_back.reshape(experts * capacity, model_width)[target].reshape(
        tok_count, top_count, model_width
    )
    grad_tokens = jnp.sum(picked_grad.astype(jnp.float32), axis=1)
    pair_summed = lax.psum_scatter(
        jnp.stack(
            [outer_rows(received, gate_delta), outer_rows(received, up_delta)], axis=1
        ).astype(jnp.bfloat16),
        "blk",
        scatter_dimension=0,
        tiled=True,
    ).astype(jnp.float32)
    grad_gate = pair_summed[:, 0]
    grad_up = pair_summed[:, 1]
    return (layer_output, grad_tokens, grad_route, grad_gate, grad_up, down_summed)


def solution(mesh):
    in_specs = (
        P(("blk", "ep"), None),
        P(("blk", "ep"), None),
        P(("blk", "ep"), None),
        P("blk", "ep", None),
        P("blk", "ep", None),
        P("blk", "ep", None),
        P(("blk", "ep"), None),
    )
    out_specs = (
        P(("blk", "ep"), None),
        P(("blk", "ep"), None),
        P(("blk", "ep"), None),
        P("blk", "ep", None),
        P("blk", "ep", None),
        P("blk", "ep", None),
    )
    return jax.shard_map(body, mesh=mesh, in_specs=in_specs, out_specs=out_specs, check_vma=False)
```

profile of v0, /device:TPU:0, one launch (start us, length us, event | category | flops | bytes accessed | tf_op | source)
XLA Modules:
  0.0 790.4 jit_solution(9528315452976201955)
XLA Ops:
  25.1 8.0 %scatter_custom_fusion = bf16[1024,1024]{1,0:T(8,128)(2,1)} fusion(s32[768]{0:T(1024)S(1)} %fusion.8, bf16[768,1024]{1,0:T(8,128)(2,1)} %reshape.126, bf16[]{:T(256)} %constant.7.clone.1), kind=kCustom, calls=%fused_computation.22 | custom fusion | bytes 2097664 | tf_op jit(solution)/shard_map/scatter | solution.py:32
  33.1 6.8 all-to-all-start
  45.9 9.6 %scatter_custom_fusion.1 = bf16[1024,1024]{1,0:T(8,128)(2,1)} fusion(s32[768]{0:T(1024)S(1)} %fusion.8, f32[768,1024]{1,0:T(8,128)S(1)} %mul.90, f32[768]{0:T(1024)S(1)} %mul.87, bf16[]{:T(256)} %constant.7.clone.1), kind=kCustom, calls=%fused_computation.19 | custom fusion | flops 1572864 | bytes 5246978 | tf_op jit(solution)/shard_map/scatter | solution.py:62
  55.5 33.6 %all-to-all-done = bf16[64,16,1024]{2,1,0:T(8,128)(2,1)} async-done(((bf16[64,16,1024]{2,1,0:T(8,128)(2,1)}), bf16[64,16,1024]{2,1,0:T(8,128)(2,1)}, u32[]{:S(2)}, u32[]{:S(2)}) %all-to-all-start) | async-done | bytes 2097184 | tf_op jit(solution)/shard_map/all_to_all | solution.py:33
  95.8 46.7 %all-to-all-done.2 = bf16[64,16,1024]{2,1,0:T(8,128)(2,1)} async-done(((bf16[64,16,1024]{2,1,0:T(8,128)(2,1)}), bf16[64,16,1024]{2,1,0:T(8,128)(2,1)}, u32[]{:S(2)}, u32[]{:S(2)}) %all-to-all-start.2) | async-done | bytes 2097184 | tf_op jit(solution)/shard_map/all_to_all | solution.py:64
  145.8 10.2 %fusion.9 = f32[8,128,768]{2,1,0:T(8,128)} fusion(bf16[8,128,1024]{2,1,0:T(8,128)(2,1)S(1)} %bitcast.68, bf16[1024,8,768]{2,0,1:T(8,128)(2,1)} %all-gather.4.cloned.1.call-done), kind=kOutput, calls=%fused_computation.36 | convolution fusion | flops 1610612736 | bytes 17825792 | tf_op jit(solution)/shard_map/erd,def->erf/dot_general | solution.py:11
  156.0 105.8 %all-gather.6.cloned.1.call-done = bf16[1024,8,768]{2,0,1:T(8,128)(2,1)} async-done(((bf16[256,8,768]{2,0,1:T(8,128)(2,1)}), bf16[1024,8,768]{2,0,1:T(8,128)(2,1)}) %all-gather.6.cloned.1.call-update) | async-done | bytes 12582928 | tf_op jit(solution)/shard_map/all_gather | solution.py:42
  261.7 8.1 %fusion.10 = f32[8,128,768]{2,1,0:T(8,128)} fusion(bf16[8,128,1024]{2,1,0:T(8,128)(2,1)S(1)} %bitcast.69, bf16[1024,8,768]{2,0,1:T(8,128)(2,1)} %all-gather.6.cloned.1.call-done), kind=kOutput, calls=%fused_computation.37 | convolution fusion | flops 1610612736 | bytes 17825792 | tf_op jit(solution)/shard_map/erd,def->erf/dot_general | solution.py:11
  269.8 116.3 %all-gather.8.cloned.1.call-done = bf16[1024,8,768]{2,0,1:T(8,128)(2,1)} async-done(((bf16[256,8,768]{2,0,1:T(8,128)(2,1)}), bf16[1024,8,768]{2,0,1:T(8,128)(2,1)}) %all-gather.8.cloned.1.call-update) | async-done | bytes 12582928 | tf_op jit(solution)/shard_map/all_gather | solution.py:43
  386.1 11.7 %multiply_convert_fusion = (bf16[8,128,768]{2,1,0:T(8,128)(2,1)}, bf16[8,128,768]{2,1,0:T(8,128)(2,1)}, bf16[8,128,768]{2,1,0:T(8,128)(2,1)S(1)}) fusion(f32[8,128,768]{2,1,0:T(8,128)} %fusion.9, f32[8,128,768]{2,1,0:T(8,128)} %fusion.10, bf16[8,128,1024]{2,1,0:T(8,128)(2,1)} %bitcast.73, bf16[1024,8,768]{2,0,1:T(8,128)(2,1)} %all-gather.8.cloned.1.call-done), kind=kOutput, calls=%fused_computation.13 | convolution fusion | flops 1623195648 | bytes 25690112 | tf_op jit(solution)/shard_map/erd,def->erf/dot_general | solution.py:11
  399.0 6.3 convert_bitcast_fusion
  405.5 8.4 %convert_bitcast_fusion.1 = bf16[1024,1,8,768]{0,3,2,1:T(8,128)(2,1)} fusion(bf16[8,128,768]{2,1,0:T(8,128)(2,1)} %get-tuple-element.28, bf16[8,128,1024]{2,1,0:T(8,128)(2,1)S(1)} %bitcast.70), kind=kOutput, calls=%fused_computation.6 | convolution fusion | flops 1616904192 | bytes 16252928 | tf_op jit(solution)/shard_map/erd,erf->def/dot_general | solution.py:19
  413.9 6.6 convert_bitcast_fusion.2
  420.5 21.0 %pad_maximum_fusion = bf16[1024,2,8,768]{0,3,2,1:T(8,128)(2,1)} fusion(bf16[1024,1,8,768]{0,3,2,1:T(8,128)(2,1)} %convert_bitcast_fusion.1, bf16[1024,1,8,768]{0,3,2,1:T(8,128)(2,1)} %convert_bitcast_fusion.2), kind=kLoop, calls=%fused_computation.4 | loop fusion | flops 12582912 | bytes 50331648 | tf_op jit(solution)/shard_map/stack | solution.py:88
  442.9 9.1 %convolution_convert_fusion = bf16[8,128,1024]{2,1,0:T(8,128)(2,1)S(1)} fusion(bf16[8,128,768]{2,1,0:T(8,128)(2,1)S(1)} %copy-done.3, bf16[1024,8,768]{2,0,1:T(8,128)(2,1)} %all-gather.8.cloned.1.call-done), kind=kOutput, calls=%fused_computation.18 | convolution fusion | flops 1611661312 | bytes 16252928 | tf_op jit(solution)/shard_map/erf,def->erd/dot_general | solution.py:15
  459.1 9.5 %fusion.11 = f32[8,128,1024]{2,1,0:T(8,128)S(1)} fusion(bf16[8,128,768]{2,1,0:T(8,128)(2,1)} %get-tuple-element.29, bf16[1024,8,768]{2,0,1:T(8,128)(2,1)} %all-gather.4.cloned.1.call-done), kind=kOutput, calls=%fused_computation.38 | convolution fusion | flops 1610612736 | bytes 18350080 | tf_op jit(solution)/shard_map/erf,def->erd/dot_general | solution.py:15
  468.6 10.7 %add_convert_fusion = bf16[8,128,1024]{2,1,0:T(8,128)(2,1)} fusion(f32[8,128,1024]{2,1,0:T(8,128)S(1)} %fusion.11, bf16[8,128,768]{2,1,0:T(8,128)(2,1)} %get-tuple-element.28, bf16[1024,8,768]{2,0,1:T(8,128)(2,1)} %all-gather.6.cloned.1.call-done), kind=kOutput, calls=%fused_computation.11 | convolution fusion | flops 1612709888 | bytes 20447232 | tf_op jit(solution)/shard_map/erf,def->erd/dot_general | solution.py:15
  483.3 24.9 %all-to-all-done.1 = bf16[8,128,1024]{2,0,1:T(8,128)(2,1)} async-done(((bf16[8,128,1024]{2,0,1:T(8,128)(2,1)}), bf16[8,128,1024]{2,0,1:T(8,128)(2,1)}, u32[]{:S(2)}, u32[]{:S(2)}) %all-to-all-start.1) | async-done | bytes 2097184 | tf_op jit(solution)/shard_map/all_to_all | solution.py:50
  523.3 38.6 %all-to-all-done.3 = bf16[8,128,1024]{2,0,1:T(8,128)(2,1)} async-done(((bf16[8,128,1024]{2,0,1:T(8,128)(2,1)}), bf16[8,128,1024]{2,0,1:T(8,128)(2,1)}, u32[]{:S(2)}, u32[]{:S(2)}) %all-to-all-start.3) | async-done | bytes 2097184 | tf_op jit(solution)/shard_map/all_to_all | solution.py:82
  588.0 163.0 %reduce-scatter.3.cloned.1.call-done = bf16[256,2,8,768]{0,3,2,1:T(8,128)(2,1)} async-done(((bf16[1024,2,8,768]{0,3,2,1:T(8,128)(2,1)}), bf16[256,2,8,768]{0,3,2,1:T(8,128)(2,1)}) %reduce-scatter.3.cloned.1.call-update) | async-done | bytes 6291472 | tf_op jit(solution)/shard_map/reduce_scatter | solution.py:87
  751.0 8.7 %convert_element_type.72 = f32[256,2,8,768]{0,3,2,1:T(8,128)} convert(bf16[256,2,8,768]{0,3,2,1:T(8,128)(2,1)} %reduce-scatter.3.cloned.1.call-done) | non-fusion elementwise | flops 3145728 | bytes 18874368 | tf_op jit(solution)/shard_map/convert_element_type | solution.py:94
  759.7 10.5 %slice_bitcast_fusion = (f32[256,8,768]{0,2,1:T(8,128)}, f32[256,8,768]{0,2,1:T(8,128)}) fusion(f32[256,2,8,768]{0,3,2,1:T(8,128)} %convert_element_type.72), kind=kLoop, calls=%fused_computation.8 | loop fusion | bytes 25165824 | tf_op jit(solution)/shard_map/squeeze | solution.py:96
  770.2 6.7 copy.63
  776.9 6.7 copy.64
  (72 shorter events, 88.7 us)
Async XLA Ops:
  7.2 138.6 %all-gather.4.cloned.1.call-start = ((), (), s32[]{:S(2)}) async-start(), calls=%async_computation.6 | async-start | bytes 15728640 | tf_op jit(solution)/shard_map/all_gather | solution.py:41
  11.4 1.9 copy-start.4
  11.4 250.3 %all-gather.6.cloned.1.call-start = ((), (), s32[]{:S(2)}) async-start(), calls=%async_computation.7 | async-start | bytes 15728640 | tf_op jit(solution)/shard_map/all_gather | solution.py:42
  15.5 1.9 copy-start.5
  15.6 370.6 %all-gather.8.cloned.1.call-start = ((), (), s32[]{:S(2)}) async-start(), calls=%async_computation.8 | async-start | bytes 15728640 | tf_op jit(solution)/shard_map/all_gather | solution.py:43
  19.7 0.7 copy-start.8
  19.7 3.5 copy-start.7
  25.1 14.9 %copy-start.6 = (bf16[128,1024]{1,0:T(8,128)(2,1)S(1)}, bf16[128,1024]{1,0:T(8,128)(2,1)}, u32[]{:S(2)}) copy-start(bf16[128,1024]{1,0:T(8,128)(2,1)} %param.13) | copy-start | bytes 786436
  33.1 56.0 %all-to-all-start = ((bf16[64,16,1024]{2,1,0:T(8,128)(2,1)}), bf16[64,16,1024]{2,1,0:T(8,128)(2,1)}, u32[]{:S(2)}, u32[]{:S(2)}) async-start(bf16[64,16,1024]{2,1,0:T(8,128)(2,1)} %bitcast.1), calls=%async_computation | async-start | bytes 4194304 | tf_op jit(solution)/shard_map/all_to_all | solution.py:33
  42.5 3.1 copy-start.9
  89.1 53.4 %all-to-all-start.2 = ((bf16[64,16,1024]{2,1,0:T(8,128)(2,1)}), bf16[64,16,1024]{2,1,0:T(8,128)(2,1)}, u32[]{:S(2)}, u32[]{:S(2)}) async-start(bf16[64,16,1024]{2,1,0:T(8,128)(2,1)} %bitcast.72), calls=%async_computation.2 | async-start | bytes 4194304 | tf_op jit(solution)/shard_map/all_to_all | solution.py:64
  93.5 488.8 %reduce-scatter.5.cloned.1.call-start = ((), (), s32[]{:S(2)}) async-start(), calls=%async_computation.10 | async-start | bytes 15728640 | tf_op jit(solution)/shard_map/reduce_scatter | solution.py:71
  386.1 12.8 %copy-start = (bf16[8,8,16,1024]{3,2,1,0:T(8,128)(2,1)S(1)}, bf16[8,8,16,1024]{3,2,1,0:T(8,128)(2,1)}, u32[]{:S(2)}) copy-start(bf16[8,8,16,1024]{3,2,1,0:T(8,128)(2,1)} %copy.56) | copy-start | bytes 6291460
  397.8 1.1 copy-start.2
  405.3 345.7 %reduce-scatter.3.cloned.1.call-start = ((), (), s32[]{:S(2)}) async-start(), calls=%async_computation.9 | async-start | bytes 31457280 | tf_op jit(solution)/shard_map/reduce_scatter | solution.py:87
  405.5 8.4 %copy-start.1 = (bf16[8,128,768]{2,1,0:T(8,128)(2,1)S(1)}, bf16[8,128,768]{2,1,0:T(8,128)(2,1)}, u32[]{:S(2)}) copy-start(bf16[8,128,768]{2,1,0:T(8,128)(2,1)} %get-tuple-element.29) | copy-start | bytes 4718596
  441.4 1.4 copy-start.3
  454.5 53.8 %all-to-all-start.1 = ((bf16[8,128,1024]{2,0,1:T(8,128)(2,1)}), bf16[8,128,1024]{2,0,1:T(8,128)(2,1)}, u32[]{:S(2)}, u32[]{:S(2)}) async-start(bf16[8,128,1024]{2,0,1:T(8,128)(2,1)} %copy.53), calls=%async_computation.1 | async-start | bytes 4194304 | tf_op jit(solution)/shard_map/all_to_all | solution.py:50
  508.2 53.6 %all-to-all-start.3 = ((bf16[8,128,1024]{2,0,1:T(8,128)(2,1)}), bf16[8,128,1024]{2,0,1:T(8,128)(2,1)}, u32[]{:S(2)}, u32[]{:S(2)}) async-start(bf16[8,128,1024]{2,0,1:T(8,128)(2,1)} %copy.57), calls=%async_computation.3 | async-start | bytes 4194304 | tf_op jit(solution)/shard_map/all_to_all | solution.py:82
Sparse Core Ops, SparseCore 0:
  11.5 125.2 all-gather.3
  139.2 122.5 all-gather.5
  263.6 122.5 all-gather.7
  405.4 120.7 reduce-scatter.4
  529.1 221.8 reduce-scatter.2
where the time goes:
time: 797 us; the launch traced here: 790 us
  waiting for transfers between devices  529 us (66%)
  local copies, waits for them, and re-layouts  94.6 us (12%)
  matrix products  80.5 us (10%)
  other arithmetic  50.8 us (6%)
  starting transfers between devices  21.3 us (3%)
  between operations  14.2 us (2%)
    reduce_scatter x1, waiting for transfers between devices, body(): lax.psum_scatter(jnp.stack([outer_rows(received, gate_delta), outer_rows(...  163 us
    all_gather x1, waiting for transfers between devices, body(): lax.all_gather(down_weight, 'blk', axis=0, tiled=True)  116 us
    all_gather x1, waiting for transfers between devices, body(): lax.all_gather(up_weight, 'blk', axis=0, tiled=True)  106 us
    all_to_all x1, waiting for transfers between devices, body(): lax.all_to_all(grad_send.reshape(experts, capacity, model_width), 'ep', s...  46.7 us
    all_to_all x1, waiting for transfers between devices, body(): lax.all_to_all(input_grad, 'ep', split_axis=1, concat_axis=0, tiled=True)  38.6 us
    unnamed x29, local copies, waits for them, and re-layouts  35.5 us
    all_to_all x1, waiting for transfers between devices, body(): lax.all_to_all(outgoing.reshape(experts, capacity, model_width), 'ep', sp...  33.6 us
    dot_general x3, matrix products, expand_rows(): jnp.einsum('erd,def->erf', routed, weights, preferred_element_type=jnp.fl...  29.9 us
  transfers between devices with their start and end apart: 9, of which 7 were waited for; matrix products, arithmetic and copies ran while one was open for 21% of the time, Pallas kernels for 0%

commit v1 on v0

--- a/solution.py
+++ b/solution.py
@@ -1,10 +1,37 @@
+import functools
 import jax
 import jax.numpy as jnp
 from jax import lax
 from jax.sharding import PartitionSpec as P
+from jax.lax import axis_index, axis_size, ppermute
 
 EXPERTS = 64
 CAP = 16
+
+
+def _apply_series(local_array, in_dim):
+    out_arr = axis_size("blk")
+    x_new = axis_index("blk")
+    r2, after, r_now = (out_arr, x_new, local_array.shape[in_dim])
+    history = [t * r2 if nth == in_dim else t for nth, t in enumerate(local_array.shape)]
+    local_part = lax.dynamic_update_slice_in_dim(
+        jnp.zeros(history, local_array.dtype), local_array, after * r_now, axis=in_dim
+    )
+    local_next = mat_out = local_array
+    for m in range(1, r2 // 2 + 1):
+        local_next = ppermute(local_next, "blk", [(nth, (nth + 1) % r2) for nth in range(r2)])
+        local_part = lax.dynamic_update_slice_in_dim(
+            local_part, local_next, (after - m) % r2 * r_now, axis=in_dim
+        )
+        if 2 * m < r2:
+            mat_out = ppermute(mat_out, "blk", [(nth, (nth - 1) % r2) for nth in range(r2)])
+            local_part = lax.dynamic_update_slice_in_dim(
+                local_part, mat_out, (after + m) % r2 * r_now, axis=in_dim
+            )
+    return local_part
+
+
+clusters_spread = functools.partial(_apply_series, in_dim=0)
 
 
 def expand_rows(routed, weights):
@@ -39,7 +66,7 @@
     )
     gate_full, up_full, down_full = (
         lax.all_gather(gate_weight, "blk", axis=0, tiled=True),
-        lax.all_gather(up_weight, "blk", axis=0, tiled=True),
+        clusters_spread(up_weight),
         lax.all_gather(down_weight, "blk", axis=0, tiled=True),
     )
     gate_pre = expand_rows(received, gate_full)

time: 797 us -> 850 us (1.066)
  waiting for transfers between devices: 529 us -> 562 us
  local copies, waits for them, and re-layouts: 94.6 us -> 116 us
    ppermute x0 -> x3, waiting for transfers between devices: none -> 298 us  [the longest x2 194 us: _apply_series(): ppermute(local_next, 'blk', [(nth, (nth + 1) % r2) for nth in range(r2)])]
    all_gather x1, waiting for transfers between devices: 116 us -> 0.01 us  [body(): lax.all_gather(down_weight, 'blk', axis=0, tiled=True)]
    all_gather x1 -> x0, waiting for transfers between devices: 106 us -> none  [body(): lax.all_gather(up_weight, 'blk', axis=0, tiled=True)]
    all_to_all x1, waiting for transfers between devices: 33.6 us -> 0.01 us  [body(): lax.all_to_all(outgoing.reshape(experts, capacity, model_width), 'ep', sp...]
    dynamic_update_slice x0 -> x4, local copies, waits for them, and re-layouts: none -> 16.7 us  [the longest x2 8.35 us: _apply_series(): lax.dynamic_update_slice_in_dim(local_part, local_next, (after - m) % r2...]
    all_to_all x1, waiting for transfers between devices: 46.7 us -> 37.7 us  [body(): lax.all_to_all(grad_send.reshape(experts, capacity, model_width), 'ep', s...]
    unnamed x29 -> x32, local copies, waits for them, and re-layouts: 35.5 us -> 33.9 us
  transfers between devices with their start and end apart: 9 -> 11, of which waited for: 7 -> 8; matrix products, arithmetic and copies ran while one was open for 21% -> 21% of each run, Pallas kernels for 0% -> 0%
where the time goes in v1:
time: 850 us; the launch traced here: 840 us
  waiting for transfers between devices  562 us (66%)
  local copies, waits for them, and re-layouts  116 us (14%)
  matrix products  73.9 us (9%)
  other arithmetic  50.5 us (6%)
  starting transfers between devices  23.4 us (3%)
  between operations  14.4 us (2%)
    ppermute x2, waiting for transfers between devices, _apply_series(): ppermute(local_next, 'blk', [(nth, (nth + 1) % r2) for nth in range(r2)])  194 us
    reduce_scatter x1, waiting for transfers between devices, body(): lax.psum_scatter(jnp.stack([outer_rows(received, gate_delta), outer_rows(...  162 us
    ppermute x1, waiting for transfers between devices, _apply_series(): ppermute(mat_out, 'blk', [(nth, (nth - 1) % r2) for nth in range(r2)])  104 us
    all_to_all x1, waiting for transfers between devices, body(): lax.all_to_all(input_grad, 'ep', split_axis=1, concat_axis=0, tiled=True)  38.7 us
    all_to_all x1, waiting for transfers between devices, body(): lax.all_to_all(grad_send.reshape(experts, capacity, model_width), 'ep', s...  37.7 us
    unnamed x32, local copies, waits for them, and re-layouts  33.9 us
    dot_general x3, matrix products, contract_rows(): jnp.einsum('erf,def->erd', inner, weights, preferred_element_type=jnp.flo...  29.3 us
    all_to_all x1, waiting for transfers between devices, body(): lax.all_to_all(expert_out, 'ep', split_axis=1, concat_axis=0, tiled=True)  24.9 us
  transfers between devices with their start and end apart: 11, of which 8 were waited for; matrix products, arithmetic and copies ran while one was open for 21% of the time, Pallas kernels for 0%

profile of v1, /device:TPU:0, one launch (start us, length us, event | category | flops | bytes accessed | tf_op | source)
XLA Modules:
  0.0 840.4 jit_solution(14204788488905423617)
XLA Ops:
  26.0 9.6 %scatter_custom_fusion.1 = bf16[1024,1024]{1,0:T(8,128)(2,1)} fusion(s32[768]{0:T(1024)S(1)} %fusion.8, f32[768,1024]{1,0:T(8,128)S(1)} %mul.106, f32[768]{0:T(1024)S(1)} %mul.103, bf16[]{:T(256)} %constant.42.clone.1), kind=kCustom, calls=%fused_computation.23 | custom fusion | flops 1572864 | bytes 5246978 | tf_op jit(solution)/shard_map/scatter | solution.py:89
  35.6 6.3 all-to-all-start.2
  45.2 8.2 scatter_custom_fusion
  53.4 37.7 %all-to-all-done.2 = bf16[64,16,1024]{2,1,0:T(8,128)(2,1)} async-done(((bf16[64,16,1024]{2,1,0:T(8,128)(2,1)}), bf16[64,16,1024]{2,1,0:T(8,128)(2,1)}, u32[]{:S(2)}, u32[]{:S(2)}) %all-to-all-start.2) | async-done | bytes 2097184 | tf_op jit(solution)/shard_map/all_to_all | solution.py:91
  97.3 76.7 %collective-permute-done = bf16[256,8,768]{2,1,0:T(8,128)(2,1)} collective-permute-done((bf16[256,8,768]{2,1,0:T(8,128)(2,1)}, bf16[256,8,768]{2,1,0:T(8,128)(2,1)}, u32[]{:S(2)}, u32[]{:S(2)}) %collective-permute-start) | collective-permute-done | bytes 3145760 | tf_op jit(solution)/shard_map/ppermute | solution.py:22
  187.7 104.2 %collective-permute-done.1 = bf16[256,8,768]{2,1,0:T(8,128)(2,1)} collective-permute-done((bf16[256,8,768]{2,1,0:T(8,128)(2,1)}, bf16[256,8,768]{2,1,0:T(8,128)(2,1)}, u32[]{:S(2)}, u32[]{:S(2)}) %collective-permute-start.1) | collective-permute-done | bytes 3145760 | tf_op jit(solution)/shard_map/ppermute | solution.py:27
  302.4 117.3 %collective-permute-done.2 = bf16[256,8,768]{2,1,0:T(8,128)(2,1)} collective-permute-done((bf16[256,8,768]{2,1,0:T(8,128)(2,1)}, bf16[256,8,768]{2,1,0:T(8,128)(2,1)}, u32[]{:S(2)}, u32[]{:S(2)}) %collective-permute-start.2) | collective-permute-done | bytes 3145760 | tf_op jit(solution)/shard_map/ppermute | solution.py:22
  423.9 8.7 %fusion.10 = f32[8,128,768]{2,1,0:T(8,128)} fusion(bf16[8,128,1024]{2,1,0:T(8,128)(2,1)} %bitcast.72, bf16[1024,8,768]{2,0,1:T(8,128)(2,1)} %all-gather.5.cloned.1.call-done), kind=kOutput, calls=%fused_computation.41 | convolution fusion | flops 1610612736 | bytes 17825792 | tf_op jit(solution)/shard_map/erd,def->erf/dot_general | solution.py:38
  433.0 8.2 fusion.9
  442.3 6.3 multiply_convert_fusion
  449.8 6.3 convert_bitcast_fusion
  456.4 8.4 convert_bitcast_fusion.1
  464.8 6.5 convert_bitcast_fusion.2
  471.3 21.0 %pad_maximum_fusion = bf16[1024,2,8,768]{0,3,2,1:T(8,128)(2,1)} fusion(bf16[1024,1,8,768]{0,3,2,1:T(8,128)(2,1)} %convert_bitcast_fusion.1, bf16[1024,1,8,768]{0,3,2,1:T(8,128)(2,1)} %convert_bitcast_fusion.2), kind=kLoop, calls=%fused_computation.4 | loop fusion | flops 12582912 | bytes 50331648 | tf_op jit(solution)/shard_map/stack | solution.py:115
  493.7 9.1 %convolution_convert_fusion = bf16[8,128,1024]{2,1,0:T(8,128)(2,1)S(1)} fusion(bf16[8,128,768]{2,1,0:T(8,128)(2,1)S(1)} %copy-done.5, bf16[1024,8,768]{2,0,1:T(8,128)(2,1)} %all-gather.5.cloned.1.call-done), kind=kOutput, calls=%fused_computation.22 | convolution fusion | flops 1611661312 | bytes 16252928 | tf_op jit(solution)/shard_map/erf,def->erd/dot_general | solution.py:42
  509.8 9.5 %fusion.11 = f32[8,128,1024]{2,1,0:T(8,128)S(1)} fusion(bf16[8,128,768]{2,1,0:T(8,128)(2,1)} %get-tuple-element.29, bf16[1024,8,768]{2,0,1:T(8,128)(2,1)} %all-gather.3.cloned.1.call-done), kind=kOutput, calls=%fused_computation.42 | convolution fusion | flops 1610612736 | bytes 18350080 | tf_op jit(solution)/shard_map/erf,def->erd/dot_general | solution.py:42
  519.4 10.7 %add_convert_fusion = bf16[8,128,1024]{2,1,0:T(8,128)(2,1)} fusion(f32[8,128,1024]{2,1,0:T(8,128)S(1)} %fusion.11, bf16[8,128,768]{2,1,0:T(8,128)(2,1)} %get-tuple-element.28, bf16[1024,8,768]{2,0,1:T(8,128)(2,1)} %copy_dynamic-update-slice_fusion), kind=kOutput, calls=%fused_computation.11 | convolution fusion | flops 1612709888 | bytes 20447232 | tf_op jit(solution)/shard_map/erf,def->erd/dot_general | solution.py:42
  534.1 24.9 %all-to-all-done.1 = bf16[8,128,1024]{2,0,1:T(8,128)(2,1)} async-done(((bf16[8,128,1024]{2,0,1:T(8,128)(2,1)}), bf16[8,128,1024]{2,0,1:T(8,128)(2,1)}, u32[]{:S(2)}, u32[]{:S(2)}) %all-to-all-start.1) | async-done | bytes 2097184 | tf_op jit(solution)/shard_map/all_to_all | solution.py:77
  573.9 38.7 %all-to-all-done.3 = bf16[8,128,1024]{2,0,1:T(8,128)(2,1)} async-done(((bf16[8,128,1024]{2,0,1:T(8,128)(2,1)}), bf16[8,128,1024]{2,0,1:T(8,128)(2,1)}, u32[]{:S(2)}, u32[]{:S(2)}) %all-to-all-start.3) | async-done | bytes 2097184 | tf_op jit(solution)/shard_map/all_to_all | solution.py:109
  638.6 162.3 %reduce-scatter.3.cloned.1.call-done = bf16[256,2,8,768]{0,3,2,1:T(8,128)(2,1)} async-done(((bf16[1024,2,8,768]{0,3,2,1:T(8,128)(2,1)}), bf16[256,2,8,768]{0,3,2,1:T(8,128)(2,1)}) %reduce-scatter.3.cloned.1.call-update) | async-done | bytes 6291472 | tf_op jit(solution)/shard_map/reduce_scatter | solution.py:114
  800.8 8.7 %convert_element_type.72 = f32[256,2,8,768]{0,3,2,1:T(8,128)} convert(bf16[256,2,8,768]{0,3,2,1:T(8,128)(2,1)} %reduce-scatter.3.cloned.1.call-done) | non-fusion elementwise | flops 3145728 | bytes 18874368 | tf_op jit(solution)/shard_map/convert_element_type | solution.py:121
  809.5 10.5 %slice_bitcast_fusion = (f32[256,8,768]{0,2,1:T(8,128)}, f32[256,8,768]{0,2,1:T(8,128)}) fusion(f32[256,2,8,768]{0,3,2,1:T(8,128)} %convert_element_type.72), kind=kLoop, calls=%fused_computation.8 | loop fusion | bytes 25165824 | tf_op jit(solution)/shard_map/squeeze | solution.py:123
  820.0 6.7 copy.72
  826.7 6.7 copy.73
  (83 shorter events, 112.6 us)
Async XLA Ops:
  7.2 416.8 %all-gather.5.cloned.1.call-start = ((), (), s32[]{:S(2)}) async-start(), calls=%async_computation.7 | async-start | bytes 15728640 | tf_op jit(solution)/shard_map/all_gather | solution.py:70
  11.4 1.9 copy-start.6
  11.4 421.6 %all-gather.3.cloned.1.call-start = ((), (), s32[]{:S(2)}) async-start(), calls=%async_computation.6 | async-start | bytes 15728640 | tf_op jit(solution)/shard_map/all_gather | solution.py:68
  15.5 0.7 copy-start.10
  15.5 3.5 copy-start.7
  21.9 3.7 copy-start.11
  35.6 7.8 copy-start.9
  35.6 55.5 %all-to-all-start.2 = ((bf16[64,16,1024]{2,1,0:T(8,128)(2,1)}), bf16[64,16,1024]{2,1,0:T(8,128)(2,1)}, u32[]{:S(2)}, u32[]{:S(2)}) async-start(bf16[64,16,1024]{2,1,0:T(8,128)(2,1)} %bitcast.75), calls=%async_computation.2 | async-start | bytes 4194304 | tf_op jit(solution)/shard_map/all_to_all | solution.py:91
  42.0 132.0 %collective-permute-start = (bf16[256,8,768]{2,1,0:T(8,128)(2,1)}, bf16[256,8,768]{2,1,0:T(8,128)(2,1)}, u32[]{:S(2)}, u32[]{:S(2)}) collective-permute-start(bf16[256,8,768]{2,1,0:T(8,128)(2,1)} %param.11), channel_id=1, source_target_pairs={{0,8},{8,16},{16,24},{24,0},{1,9},{9,17},{17,25},{25,1},{2,10},{10... | collective-permute-start | bytes 9437192 | tf_op jit(solution)/shard_map/ppermute | solution.py:22
  91.1 208.2 %all-to-all-start = ((bf16[64,16,1024]{2,1,0:T(8,128)(2,1)}), bf16[64,16,1024]{2,1,0:T(8,128)(2,1)S(1)}, u32[]{:S(2)}, u32[]{:S(2)}) async-start(bf16[64,16,1024]{2,1,0:T(8,128)(2,1)} %bitcast.1), calls=%async_computation | async-start | bytes 4194304 | tf_op jit(solution)/shard_map/all_to_all | solution.py:60
  94.7 538.1 %reduce-scatter.5.cloned.1.call-start = ((), (), s32[]{:S(2)}) async-start(), calls=%async_computation.9 | async-start | bytes 15728640 | tf_op jit(solution)/shard_map/reduce_scatter | solution.py:98
  94.8 197.1 %collective-permute-start.1 = (bf16[256,8,768]{2,1,0:T(8,128)(2,1)}, bf16[256,8,768]{2,1,0:T(8,128)(2,1)}, u32[]{:S(2)}, u32[]{:S(2)}) collective-permute-start(bf16[256,8,768]{2,1,0:T(8,128)(2,1)} %param.11), channel_id=1, source_target_pairs={{0,24},{8,0},{16,8},{24,16},{1,25},{9,1},{17,9},{25,17},{2,26},{10... | collective-permute-start | bytes 9437192 | tf_op jit(solution)/shard_map/ppermute | solution.py:27
  173.9 245.8 %collective-permute-start.2 = (bf16[256,8,768]{2,1,0:T(8,128)(2,1)}, bf16[256,8,768]{2,1,0:T(8,128)(2,1)}, u32[]{:S(2)}, u32[]{:S(2)}) collective-permute-start(bf16[256,8,768]{2,1,0:T(8,128)(2,1)} %collective-permute-done), channel_id=1, source_target_pairs={{0,8},{8,16},{16,24},{24,0},{1,9},{9,17},{17,25},{25,1},{2,10},{10... | collective-permute-start | bytes 9437192 | tf_op jit(solution)/shard_map/ppermute | solution.py:22
  299.3 1.3 copy-start.2
  433.0 9.3 %copy-start = (bf16[1024,8,768]{2,0,1:T(8,128)(2,1)S(1)}, bf16[1024,8,768]{2,0,1:T(8,128)(2,1)}, u32[]{:S(2)}) copy-start(bf16[1024,8,768]{2,0,1:T(8,128)(2,1)} %copy_dynamic-update-slice_fusion) | copy-start | bytes 37748740
  442.3 7.5 copy-start.1
  448.6 1.1 copy-start.4
  456.1 344.7 %reduce-scatter.3.cloned.1.call-start = ((), (), s32[]{:S(2)}) async-start(), calls=%async_computation.8 | async-start | bytes 31457280 | tf_op jit(solution)/shard_map/reduce_scatter | solution.py:114
  456.4 8.4 %copy-start.3 = (bf16[8,128,768]{2,1,0:T(8,128)(2,1)S(1)}, bf16[8,128,768]{2,1,0:T(8,128)(2,1)}, u32[]{:S(2)}) copy-start(bf16[8,128,768]{2,1,0:T(8,128)(2,1)} %get-tuple-element.29) | copy-start | bytes 4718596
  492.3 1.4 copy-start.5
  505.3 53.7 %all-to-all-start.1 = ((bf16[8,128,1024]{2,0,1:T(8,128)(2,1)}), bf16[8,128,1024]{2,0,1:T(8,128)(2,1)}, u32[]{:S(2)}, u32[]{:S(2)}) async-start(bf16[8,128,1024]{2,0,1:T(8,128)(2,1)} %copy.62), calls=%async_computation.1 | async-start | bytes 4194304 | tf_op jit(solution)/shard_map/all_to_all | solution.py:77
  534.1 29.5 %copy-start.8 = (bf16[128,1024]{1,0:T(8,128)(2,1)S(1)}, bf16[128,1024]{1,0:T(8,128)(2,1)}, u32[]{:S(2)}) copy-start(bf16[128,1024]{1,0:T(8,128)(2,1)} %param.13) | copy-start | bytes 786436
  559.0 53.7 %all-to-all-start.3 = ((bf16[8,128,1024]{2,0,1:T(8,128)(2,1)}), bf16[8,128,1024]{2,0,1:T(8,128)(2,1)}, u32[]{:S(2)}, u32[]{:S(2)}) async-start(bf16[8,128,1024]{2,0,1:T(8,128)(2,1)} %copy.66), calls=%async_computation.3 | async-start | bytes 4194304 | tf_op jit(solution)/shard_map/all_to_all | solution.py:109
Sparse Core Ops, SparseCore 0:
  11.5 207.8 all-gather.4
  221.8 211.1 all-gather.2
  456.2 119.7 reduce-scatter.4
  579.0 221.8 reduce-scatter.2
